TPU v7x, 256 devices: a whole 4x4x8 slice. The times are simulated.
256 devices in a mesh: seq: 64 (over z, y, core), slide: 4 (over x).
Axes of the slice: x: 4, y: 4, z: 8, core: 2. Of those that a mesh axis runs over, the one named last changes fastest.
Arguments:
- queries: bfloat16 [4, 8192, 768], P('slide', 'seq'), may hold values from -36 to 36
- keys: bfloat16 [4, 8192, 768], P('slide', 'seq'), may hold values from -6 to 6
- values: bfloat16 [4, 8192, 768], P('slide', 'seq'), may hold values from -6 to 6
- grad_out: bfloat16 [4, 8192, 768], P('slide', 'seq'), may hold values from -96 to 96
- w_out: bfloat16 [768, 768], replicated, may hold values from -0.21875 to 0.21875
- kept_tiles: int32 [4], P('slide'), may hold values from 2048 to 8192, as said below
Outputs:
- d_queries: bfloat16 [4, 8192, 768], P('slide', 'seq')
- d_keys: bfloat16 [4, 8192, 768], P('slide', 'seq')
- d_values: bfloat16 [4, 8192, 768], P('slide', 'seq')
- d_w_out: float32 [768, 768], replicated
Inputs may be any that keep to these rules, and one draw needn't show every extreme that they name: `kept_tiles`: at least one slide keeps all 8192 positions.
All inputs are finite; a program needn't handle non-finite values.
Results may differ from a plain program's by a relative error of at most 0.023.
Values may be sent and summed in bfloat16 or wider, within the bound.
A program may use at most 64 MiB of HBM per device.

v0:
```python
import jax
import jax.numpy as jnp
from jax import lax
from jax.sharding import PartitionSpec as P

HEADS = 16
DILATION_RATE = 16


def from_partner(block, axis, apart):
    count = lax.axis_size(axis)
    route = []
    for low in range(count):
        high = low | 1 << apart
        if high != low and high < count:
            route += [(low, high), (high, low)]
    return lax.ppermute(block, axis, route)


def head_pass(query_rows, key_rows, value_rows, grad_rows, key_valid, row_valid, scaling):
    scores = (
        jnp.einsum("qhd,khd->hqk", query_rows, key_rows, preferred_element_type=jnp.float32)
        * scaling
    )
    scores = jnp.where(key_valid[:, None, :], scores, -1e30)
    row_max = jnp.max(scores, axis=-1, keepdims=True)
    log_norm = row_max + jnp.log(jnp.sum(jnp.exp(scores - row_max), axis=-1, keepdims=True))
    probs = jnp.exp(scores - log_norm)
    probs_low = probs.astype(jnp.bfloat16)
    mixed = jnp.einsum("hqk,khd->qhd", probs_low, value_rows, preferred_element_type=jnp.float32)
    attn_low = (mixed * row_valid[:, :, None]).astype(jnp.bfloat16)
    d_probs = jnp.einsum("qhd,khd->hqk", grad_rows, value_rows, preferred_element_type=jnp.float32)
    row_dot = jnp.transpose(
        jnp.sum(grad_rows.astype(jnp.float32) * attn_low.astype(jnp.float32), axis=-1)
    )[:, :, None]
    d_scores = (probs * (d_probs - row_dot)).astype(jnp.bfloat16)
    d_query = (
        jnp.einsum("hqk,khd->qhd", d_scores, key_rows, preferred_element_type=jnp.float32) * scaling
    )
    d_key = (
        jnp.einsum("hqk,qhd->khd", d_scores, query_rows, preferred_element_type=jnp.float32)
        * scaling
    )
    d_value = jnp.einsum("hqk,qhd->khd", probs_low, grad_rows, preferred_element_type=jnp.float32)
    return (attn_low, log_norm, row_dot, d_query, d_key, d_value, probs_low, d_scores)


def dilated_rows(tile_block, heads_of_group):
    group_layout = tile_block.reshape(
        tile_block.shape[0] // DILATION_RATE, DILATION_RATE, heads_of_group, -1
    )
    return jnp.stack([group_layout[:, head, head] for head in range(heads_of_group)], axis=1)


def spread_rows(selected_rows, heads_of_group):
    indicator_matrix = (
        jnp.arange(DILATION_RATE)[:, None] == jnp.arange(heads_of_group)[None, :]
    ).astype(selected_rows.dtype)
    complete_rows = selected_rows[:, None, :, :] * indicator_matrix[None, :, :, None]
    return complete_rows.reshape(selected_rows.shape[0] * DILATION_RATE, -1)


def per_device(queries, keys, values, grad_out, w_out, kept_tiles):
    query_all = queries[0]
    key_all = keys[0]
    value_all = values[0]
    grad_all = grad_out[0]
    kept_count = kept_tiles[0]
    nearby_rows, features = query_all.shape
    head_dim = features // HEADS
    half_width = features // 2
    heads_of_group = HEADS // 2
    scaling = head_dim ** (-0.5)
    shard_index = lax.axis_index("seq")
    token_positions = shard_index * nearby_rows + jnp.arange(nearby_rows)
    row_valid = (token_positions < kept_count).astype(jnp.float32)
    d_attn = (
        lax.dot_general(
            grad_all, w_out, (((1,), (1,)), ((), ())), preferred_element_type=jnp.float32
        )
        * row_valid[:, None]
    ).astype(jnp.bfloat16)
    bit_order = [0, 1]
    keys_values = jnp.concatenate([key_all[:, :half_width], value_all[:, :half_width]], axis=1)
    block_ids = [shard_index]
    for which_bit in bit_order:
        received = from_partner(keys_values, "seq", which_bit)
        keys_values = jnp.concatenate([keys_values, received], axis=0)
        block_ids = block_ids + [
            jnp.bitwise_xor(tile_block, 1 << which_bit) for tile_block in block_ids
        ]
    key_positions = jnp.concatenate(
        [tile_block * nearby_rows + jnp.arange(nearby_rows) for tile_block in block_ids]
    )
    key_valid = (key_positions < kept_count)[None, :]
    segment_rows = keys_values.shape[0]
    near_keys = keys_values[:, :half_width].reshape(segment_rows, heads_of_group, head_dim)
    near_values = keys_values[:, half_width:].reshape(segment_rows, heads_of_group, head_dim)
    near_queries = query_all[:, :half_width].reshape(nearby_rows, heads_of_group, head_dim)
    near_grads = d_attn[:, :half_width].reshape(nearby_rows, heads_of_group, head_dim)
    pieces = []
    for first_head in range(0, heads_of_group, 2):
        pieces.append(
            head_pass(
                near_queries[:, first_head : first_head + 2],
                near_keys[:, first_head : first_head + 2],
                near_values[:, first_head : first_head + 2],
                near_grads[:, first_head : first_head + 2],
                key_valid,
                row_valid[:, None],
                scaling,
            )
        )
    attn_near = jnp.concatenate([piece[0] for piece in pieces], axis=1).reshape(
        nearby_rows, half_width
    )
    dq_near = jnp.concatenate([piece[3] for piece in pieces], axis=1).reshape(
        nearby_rows, half_width
    )
    near_terms = jnp.concatenate(
        [
            jnp.concatenate([piece[4] for piece in pieces], axis=1).reshape(
                segment_rows, half_width
            ),
            jnp.concatenate([piece[5] for piece in pieces], axis=1).reshape(
                segment_rows, half_width
            ),
        ],
        axis=1,
    )
    for which_bit in reversed(bit_order):
        middle = near_terms.shape[0] // 2
        returned = from_partner(near_terms[middle:], "seq", which_bit)
        near_terms = near_terms[:middle] + returned
    selected_row_index = nearby_rows // DILATION_RATE
    far_queries = dilated_rows(query_all[:, half_width:], heads_of_group)
    own_keys = dilated_rows(key_all[:, half_width:], heads_of_group)
    own_values = dilated_rows(value_all[:, half_width:], heads_of_group)
    far_grads = dilated_rows(d_attn[:, half_width:], heads_of_group)
    selected_positions = (
        token_positions[::DILATION_RATE][:, None] + jnp.arange(heads_of_group)[None, :]
    )
    sel_valid = selected_positions < kept_count
    far_keys, far_values = (
        lax.all_gather(own_keys.reshape(selected_row_index, half_width), "seq", axis=0, tiled=True),
        lax.all_gather(
            own_values.reshape(selected_row_index, half_width), "seq", axis=0, tiled=True
        ),
    )
    distant_count = far_keys.shape[0]
    distant_positions = (
        jnp.arange(distant_count)[:, None] * DILATION_RATE + jnp.arange(heads_of_group)[None, :]
    )
    far_valid = jnp.transpose(distant_positions < kept_count)
    far_out = head_pass(
        far_queries,
        far_keys.reshape(distant_count, heads_of_group, head_dim),
        far_values.reshape(distant_count, heads_of_group, head_dim),
        far_grads,
        far_valid,
        sel_valid.astype(jnp.float32),
        scaling,
    )
    attn_far, log_norm, row_dot, dq_far = (far_out[0], far_out[1], far_out[2], far_out[3])
    all_queries, all_grads = (
        lax.all_gather(
            far_queries.reshape(selected_row_index, half_width), "seq", axis=0, tiled=True
        ),
        lax.all_gather(
            far_grads.reshape(selected_row_index, half_width), "seq", axis=0, tiled=True
        ),
    )
    all_norms, all_dots = (
        lax.all_gather(jnp.transpose(log_norm[:, :, 0]), "seq", axis=0, tiled=True),
        lax.all_gather(jnp.transpose(row_dot[:, :, 0]), "seq", axis=0, tiled=True),
    )
    query_rows = all_queries.reshape(distant_count, heads_of_group, head_dim)
    grad_rows = all_grads.reshape(distant_count, heads_of_group, head_dim)
    scores = (
        jnp.einsum("qhd,khd->hqk", query_rows, own_keys, preferred_element_type=jnp.float32)
        * scaling
    )
    scores = jnp.where(jnp.transpose(sel_valid)[:, None, :], scores, -1e30)
    probs = jnp.exp(scores - jnp.transpose(all_norms)[:, :, None])
    probs_back = probs.astype(jnp.bfloat16)
    d_probs = jnp.einsum("qhd,khd->hqk", grad_rows, own_values, preferred_element_type=jnp.float32)
    d_back = (probs * (d_probs - jnp.transpose(all_dots)[:, :, None])).astype(jnp.bfloat16)
    d_key = (
        jnp.einsum("hqk,qhd->khd", d_back, query_rows, preferred_element_type=jnp.float32) * scaling
    )
    d_value = jnp.einsum("hqk,qhd->khd", probs_back, grad_rows, preferred_element_type=jnp.float32)
    own_terms = jnp.concatenate(
        [
            d_key.reshape(selected_row_index, half_width),
            d_value.reshape(selected_row_index, half_width),
        ],
        axis=1,
    )
    dk_far = own_terms[:, :half_width].reshape(selected_row_index, heads_of_group, head_dim)
    dv_far = own_terms[:, half_width:].reshape(selected_row_index, heads_of_group, head_dim)
    attn = jnp.concatenate([attn_near, spread_rows(attn_far, heads_of_group)], axis=1)
    weight_scale = (nearby_rows * lax.axis_size("seq") * lax.axis_size("slide")) ** (-0.5)
    weight_term = (
        lax.dot_general(
            attn, grad_all, (((0,), (0,)), ((), ())), preferred_element_type=jnp.float32
        )
        * weight_scale
    )
    weight_sum = lax.psum(weight_term, ("seq", "slide"))
    d_queries = jnp.concatenate([dq_near, spread_rows(dq_far, heads_of_group)], axis=1).astype(
        jnp.bfloat16
    )
    d_keys = jnp.concatenate(
        [near_terms[:, :half_width], spread_rows(dk_far, heads_of_group)], axis=1
    ).astype(jnp.bfloat16)
    d_values = jnp.concatenate(
        [near_terms[:, half_width:], spread_rows(dv_far, heads_of_group)], axis=1
    ).astype(jnp.bfloat16)
    return (d_queries[None], d_keys[None], d_values[None], weight_sum)


def solution(mesh):
    in_specs = (
        P("slide", "seq", None),
        P("slide", "seq", None),
        P("slide", "seq", None),
        P("slide", "seq", None),
        P(),
        P("slide"),
    )
    out_specs = (P("slide", "seq", None), P("slide", "seq", None), P("slide", "seq", None), P())
    return jax.shard_map(
        per_device, mesh=mesh, in_specs=in_specs, out_specs=out_specs, check_vma=False
    )
```

profile of v0, /device:TPU:1, one launch (start us, length us, event | category | flops | bytes accessed | tf_op | source)
XLA Modules:
  0.0 602.9 jit_solution(7452055038096402020)
XLA Ops:
  7.2 1.2 fusion.103
  8.4 0.7 pad_maximum_fusion.5
  9.1 3.2 collective-permute-start
  13.3 1.5 fusion.16
  14.8 0.7 fusion.101
  15.4 0.2 reshape.385
  15.9 0.2 reshape.386
  16.4 50.6 %all_gather.22 = bf16[512,384]{1,0:T(8,128)(2,1)S(1)} all-gather(bf16[8,384]{1,0:T(8,128)(2,1)S(1)} %reshape.394), channel_id=1, replica_groups=mesh['seq'=64,'slide'=4] {'seq'}, dimensions={0}, use_global_device_ids=true | all-gather | bytes 399360 | tf_op jit(solution)/shard_map/all_gather | solution.py:169
  67.2 46.9 %all_gather.20 = bf16[512,384]{1,0:T(8,128)(2,1)S(1)} all-gather(bf16[8,384]{1,0:T(8,128)(2,1)S(1)} %reshape.392), channel_id=1, replica_groups=mesh['seq'=64,'slide'=4] {'seq'}, dimensions={0}, use_global_device_ids=true | all-gather | bytes 399360 | tf_op jit(solution)/shard_map/all_gather | solution.py:166
  114.3 0.2 reshape.382
  114.8 0.2 reshape.387
  115.3 46.9 %all_gather.19 = bf16[512,384]{1,0:T(8,128)(2,1)S(1)} all-gather(bf16[8,384]{1,0:T(8,128)(2,1)S(1)} %reshape.388), channel_id=1, replica_groups=mesh['seq'=64,'slide'=4] {'seq'}, dimensions={0}, use_global_device_ids=true | all-gather | bytes 399360 | tf_op jit(solution)/shard_map/all_gather | solution.py:146
  162.4 47.1 %all_gather.18 = bf16[512,384]{1,0:T(8,128)(2,1)S(1)} all-gather(bf16[8,384]{1,0:T(8,128)(2,1)S(1)} %reshape.383), channel_id=1, replica_groups=mesh['seq'=64,'slide'=4] {'seq'}, dimensions={0}, use_global_device_ids=true | all-gather | bytes 399360 | tf_op jit(solution)/shard_map/all_gather | solution.py:145
  209.7 0.2 fusion.105
  210.2 0.3 multiply_reduce_fusion.4
  210.6 0.3 fusion.40
  210.9 42.0 %all_gather.23 = f32[512,8]{1,0:T(8,128)S(1)} all-gather(f32[8,8]{1,0:T(8,128)S(1)} %copy.344), channel_id=1, replica_groups=mesh['seq'=64,'slide'=4] {'seq'}, dimensions={0}, use_global_device_ids=true | all-gather | bytes 16640 | tf_op jit(solution)/shard_map/all_gather | solution.py:175
  253.0 43.4 %all_gather.21 = f32[512,8]{1,0:T(8,128)S(1)} all-gather(f32[8,8]{1,0:T(8,128)S(1)} %copy.340), channel_id=1, replica_groups=mesh['seq'=64,'slide'=4] {'seq'}, dimensions={0}, use_global_device_ids=true | all-gather | bytes 16640 | tf_op jit(solution)/shard_map/all_gather | solution.py:174
  296.8 0.3 fusion.42
  297.6 0.8 mul.341
  298.5 1.0 pad_maximum_fusion.4
  299.4 0.3 collective-permute-start.1
  299.7 0.3 multiply_convert_fusion
  300.0 0.8 concatenate.96
  300.8 0.8 concatenate.93
  301.7 0.8 concatenate.87
  302.5 7.7 %collective-permute-done.1 = bf16[256,768]{1,0:T(8,128)(2,1)S(1)} collective-permute-done((bf16[256,768]{1,0:T(8,128)(2,1)S(1)}, bf16[256,768]{1,0:T(8,128)(2,1)S(1)}, u32[]{:S(2)}, u32[]{:S(2)}) %collective-permute-start.1) | collective-permute-done | bytes 393248 | tf_op jit(solution)/shard_map/ppermute | solution.py:17
  310.2 1.0 pad_maximum_fusion.1
  311.2 0.8 fusion.96
  312.2 0.3 fusion.107
  312.5 0.3 fusion.108
  312.8 1.2 copy.277
  314.7 0.8 fusion.48
  315.8 0.3 fusion.109
  316.7 0.3 fusion.106
  317.4 0.8 multiply_reduce_fusion.3
  318.2 0.3 fusion.14
  318.5 1.0 fusion.13
  319.5 1.0 fusion.12
  320.5 1.0 fusion.15
  321.5 0.3 copy.336
  321.8 0.6 copy-done.4
  322.3 1.2 fusion.20
  323.5 1.1 fusion.17
  325.1 1.0 pad_maximum_fusion.2
  326.1 1.4 copy.335
  327.5 0.7 pad_maximum_fusion.10
  328.2 1.0 copy.349
  329.2 0.9 pad_maximum_fusion
  330.2 0.3 collective-permute-start.2
  330.4 1.9 convolution_multiply_fusion
  332.4 1.1 fusion.51
  333.5 1.1 fusion.45
  334.6 1.1 fusion.47
  335.7 13.2 %collective-permute-done.2 = f32[256,768]{1,0:T(8,128)} collective-permute-done((f32[256,768]{1,0:T(8,128)}, f32[256,768]{1,0:T(8,128)}, u32[]{:S(2)}, u32[]{:S(2)}) %collective-permute-start.2) | collective-permute-done | bytes 786464 | tf_op jit(solution)/shard_map/ppermute | solution.py:17
  349.0 1.2 fusion.54
  350.2 2.2 collective-permute-start.3
  352.8 0.7 pad_maximum_fusion.6
  353.5 0.3 collective-permute-done.3
  353.8 1.0 fusion.59
  354.9 0.7 pad_maximum_fusion.8
  355.6 0.7 pad_maximum_fusion.7
  356.3 236.5 %all-reduce.2.cloned.1.call-done = f32[768,768]{1,0:T(8,128)} async-done(((f32[768,768]{1,0:T(8,128)}), f32[768,768]{1,0:T(8,128)}) %all-reduce.2.cloned.1.call-update) | async-done | bytes 2359312 | tf_op jit(solution)/shard_map/psum | solution.py:209
  592.8 3.2 copy.526
  (138 shorter events, 6.1 us)
Async XLA Ops:
  7.2 6.1 %copy-start = (bf16[768,768]{1,0:T(8,128)(2,1)S(1)}, bf16[768,768]{1,0:T(8,128)(2,1)}, u32[]{:S(2)}) copy-start(bf16[768,768]{1,0:T(8,128)(2,1)} %param.10) | copy-start | bytes 3538948
  7.2 585.6 %all-reduce.2.cloned.1.call-start = ((), (), s32[]{:S(2)}) async-start(), calls=%async_computation | async-start | bytes 4718592 | tf_op jit(solution)/shard_map/psum | solution.py:209
  7.2 7.5 %copy-start.13 = (bf16[1,128,768]{2,1,0:T(8,128)(2,1)S(1)}, bf16[1,128,768]{2,1,0:T(8,128)(2,1)}, u32[]{:S(2)}) copy-start(bf16[1,128,768]{2,1,0:T(8,128)(2,1)} %param.6) | copy-start | bytes 589828
  9.1 289.3 %collective-permute-start = (bf16[128,768]{1,0:T(8,128)(2,1)}, bf16[128,768]{1,0:T(8,128)(2,1)}, u32[]{:S(2)}, u32[]{:S(2)}) collective-permute-start(bf16[128,768]{1,0:T(8,128)(2,1)} %pad_maximum_fusion.5), channel_id=1, source_target_pairs={{0,4},{4,0},{8,12},{12,8},{16,20},{20,16},{24,28},{28,24},{32,36},... | collective-permute-start | bytes 589832 | tf_op jit(solution)/shard_map/ppermute | solution.py:17
  13.0 301.1 %copy-start.15 = (f32[128]{0:T(128)}, f32[128]{0:T(128)S(1)}, u32[]{:S(2)}) copy-start(f32[128]{0:T(128)S(1)} %compare_convert_fusion) | copy-start | bytes 1540
  253.0 44.4 %copy-start.7 = (bf16[128,384]{1,0:T(8,128)(2,1)S(1)}, bf16[128,384]{1,0:T(8,128)(2,1)}, u32[]{:S(2)}) copy-start(bf16[128,384]{1,0:T(8,128)(2,1)} %get-tuple-element.44) | copy-start | bytes 294916
  297.6 19.1 %copy-start.3 = (bf16[128,384]{0,1:T(8,128)(2,1)}, bf16[128,384]{0,1:T(8,128)(2,1)S(1)}, u32[]{:S(2)}) copy-start(bf16[128,384]{0,1:T(8,128)(2,1)S(1)} %copy.275) | copy-start | bytes 294916
  299.4 10.8 %collective-permute-start.1 = (bf16[256,768]{1,0:T(8,128)(2,1)S(1)}, bf16[256,768]{1,0:T(8,128)(2,1)S(1)}, u32[]{:S(2)}, u32[]{:S(2)}) collective-permute-start(bf16[256,768]{1,0:T(8,128)(2,1)S(1)} %pad_maximum_fusion.4), channel_id=1, source_target_pairs={{0,8},{8,0},{4,12},{12,4},{16,24},{24,16},{20,28},{28,20},{32,40},... | collective-permute-start | bytes 1179656 | tf_op jit(solution)/shard_map/ppermute | solution.py:17
  302.5 13.2 %copy-start.17 = (pred[512]{0:T(512)(128)(4,1)}, pred[512]{0:T(512)(128)(4,1)S(1)}, u32[]{:S(2)}) copy-start(pred[512]{0:T(512)(128)(4,1)S(1)} %add_compare_fusion.3) | copy-start | bytes 1540
  314.7 1.5 copy-start.16
  316.1 0.7 copy-start.18
  316.4 1.8 copy-start.11
  321.4 0.9 copy-start.4
  322.3 2.6 copy-start.2
  325.1 2.4 copy-start.12
  325.1 2.4 copy-start.14
  329.2 1.2 copy-start.5
  329.2 1.2 copy-start.6
  330.2 18.8 %collective-permute-start.2 = (f32[256,768]{1,0:T(8,128)}, f32[256,768]{1,0:T(8,128)}, u32[]{:S(2)}, u32[]{:S(2)}) collective-permute-start(f32[256,768]{1,0:T(8,128)} %pad_maximum_fusion), channel_id=1, source_target_pairs={{0,8},{8,0},{4,12},{12,4},{16,24},{24,16},{20,28},{28,20},{32,40},... | collective-permute-start | bytes 2359304 | tf_op jit(solution)/shard_map/ppermute | solution.py:17
  350.2 2.5 copy-start.1
  350.2 2.6 copy-start.10
  350.2 4.7 copy-start.9
  350.2 5.4 copy-start.8
  350.2 3.6 collective-permute-start.3
Sparse Core Ops, SparseCore 0:
  332.5 260.2 all-reduce.1
where the time goes:
time: 604 us; the launch traced here: 603 us
  blocking collectives  277 us (46%)
  waiting for transfers between devices  258 us (43%)
  matrix products  18.6 us (3%)
  local copies, waits for them, and re-layouts  17.4 us (3%)
  between operations  15.5 us (3%)
  other arithmetic  10.7 us (2%)
    psum x1, waiting for transfers between devices, per_device(): weight_sum = lax.psum(weight_term, ('seq', 'slide'))  236 us
    all_gather x1, blocking collectives, per_device(): lax.all_gather(far_grads.reshape(selected_row_index, half_width), 'seq',...  50.6 us
    all_gather x1, blocking collectives, per_device(): lax.all_gather(own_keys.reshape(selected_row_index, half_width), 'seq', a...  47.1 us
    all_gather x1, blocking collectives, per_device(): lax.all_gather(far_queries.reshape(selected_row_index, half_width), 'seq'...  46.9 us
    all_gather x1, blocking collectives, per_device(): lax.all_gather(own_values.reshape(selected_row_index, half_width), 'seq',...  46.9 us
    all_gather x1, blocking collectives, per_device(): lax.all_gather(jnp.transpose(log_norm[:, :, 0]), 'seq', axis=0, tiled=True)  43.4 us
    all_gather x1, blocking collectives, per_device(): lax.all_gather(jnp.transpose(row_dot[:, :, 0]), 'seq', axis=0, tiled=True)  42 us
    ppermute x4, waiting for transfers between devices, from_partner(): return lax.ppermute(block, axis, route)  21.3 us
  transfers between devices with their start and end apart: 5, of which 4 were waited for; matrix products, arithmetic and copies ran while one was open for 3% of the time, Pallas kernels for 0%

commit v1 on v0

v1 whole, which is shorter than its diff:
```python
import jax
import jax.numpy as jnp
from jax import lax
from jax.experimental import pallas as pl
from jax.experimental.pallas import tpu as pltpu
from jax.sharding import PartitionSpec as P

ROWS = 128
WIDTH = 768
HALF = 384
HD = 48
SEG = 512
F32 = jnp.float32
BF16 = jnp.bfloat16
MESH = pl.DeviceIdType.MESH
NN = (((1,), (0,)), ((), ()))
NT = (((1,), (1,)), ((), ()))


def dot(a, b, dims=NN):
    return lax.dot_general(a, b, dims, preferred_element_type=F32)


def iota(shape, dim):
    return lax.broadcasted_iota(jnp.int32, shape, dim)


def one_hot(mask):
    return jnp.where(mask, 1.0, 0.0).astype(BF16)


def turn(a):
    return jnp.transpose(a.astype(F32)).astype(BF16)


def head_pass(q_t, k_t, v_t, o_t, key_ok, row_ok):
    scaling = HD ** -0.5
    scores = dot(turn(k_t), q_t) * scaling
    scores = jnp.where(key_ok, scores, -1e30)
    top = jnp.max(scores, axis=0, keepdims=True)
    grown = jnp.exp(scores - top)
    probs = grown * (1.0 / jnp.sum(grown, axis=0, keepdims=True))
    low = probs.astype(BF16)
    attn = (dot(v_t, low) * row_ok).astype(BF16)
    d_probs = dot(turn(v_t), o_t)
    row_dot = jnp.sum(o_t.astype(F32) * attn.astype(F32), axis=0, keepdims=True)
    d_scores = (probs * (d_probs - row_dot)).astype(BF16)
    d_q = (dot(k_t, d_scores) * scaling).astype(BF16)
    d_k = (dot(q_t, d_scores, NT) * scaling).astype(BF16)
    d_v = dot(o_t, low, NT).astype(BF16)
    return attn, d_q, d_k, d_v


def owner_of(j):
    return 8 * j + 2 * (j % 4) + j // 4


def kernel(
    kept_ref, q_ref, k_ref, v_ref, g_ref, w_ref,
    dq_ref, dk_ref, dv_ref, dw_ref,
    a_send, a_recv, a_back, a_ret, b_send, b_recv, b_back, b_ret,
    part, c_send, c_recv, h_ref, s1_send, s1_recv, s2_own, s2_send, s2_recv,
    z_buf, g1, g2, g3,
    a_ss, a_rs, ar_ss, ar_rs, b_ss, b_rs, br_ss, br_rs, c_ss, c_rs,
    s1_ss, s1_rs, s2_ss, s2_rs, z_ss, z_rs, g1_ss, g1_rs, g2_ss, g2_rs, g3_ss, g3_rs,
):
    seq = lax.axis_index("seq")
    x = lax.axis_index("slide")
    core = seq % 2
    y = (seq // 2) % 4
    z = seq // 8
    pos = seq % 4
    first = seq - pos
    is_owner = seq == owner_of(z)

    def x_peer(r):
        return (seq, (x + r) % 4)

    def y_peer(r):
        return ((z * 4 + (y + r) % 4) * 2 + core, x)

    def z_peer(r):
        return ((((z + r) % 8) * 4 + y) * 2 + core, x)

    partner = (seq + 1 - 2 * core, x)

    def send(src, dst, ss, rs, device):
        copy = pltpu.make_async_remote_copy(
            src_ref=src, dst_ref=dst, send_sem=ss, recv_sem=rs,
            device_id=device, device_id_type=MESH,
        )
        copy.start()
        return copy

    barrier = pltpu.get_barrier_semaphore()

    def greet(device):
        pl.semaphore_signal(barrier, inc=1, device_id=device, device_id_type=MESH)

    greet(partner)
    for r in range(1, 4):
        greet((first + (pos + r) % 4, x))
        greet(x_peer(r))
        greet(y_peer(r))
    for r in range(1, 8):
        greet(z_peer(r))

    def greet_owner(j, carry):
        @pl.when(owner_of(j) != seq)
        def _():
            greet((owner_of(j), x))
        return carry

    lax.fori_loop(0, 8, greet_owner, 0)

    @pl.when(is_owner)
    def _():
        def greet_all(r, carry):
            greet(((seq + r) % 64, x))
            return carry
        lax.fori_loop(1, 64, greet_all, 0)

    kept = kept_ref[0]
    half = pl.ds(HALF, HALF)

    col_ok = jnp.where(seq * ROWS + iota((1, ROWS), 1) < kept, 1.0, 0.0)
    grad = g_ref[...]
    d_attn = (dot(w_ref[...], grad, NT) * col_ok).astype(BF16)
    near = (turn(q_ref[:, :HALF]), turn(k_ref[:, :HALF]), turn(v_ref[:, :HALF]), d_attn[:HALF])
    for d in range(4):
        for t in range(4):
            a_send[d, 96 * t : 96 * t + 96, :] = near[t][96 * d : 96 * d + 96]
    a_recv[pos] = a_send[pos]

    r64 = iota((64, ROWS), 0)
    pick = one_hot(iota((64, ROWS), 1) == 16 * (r64 & 7) + (r64 >> 3))
    l_in = iota((64, HALF), 1) - HD * (iota((64, HALF), 0) >> 3)
    own_lanes = (l_in >= 0) & (l_in < HD)
    feat = iota((HALF, ROWS), 0)
    feat = feat - HD * ((feat * 683) >> 15)
    lane = iota((HALF, ROWS), 1)
    fold0 = one_hot(lane == feat)
    fold1 = one_hot(lane == feat + HD)

    def far(block, dims=NN):
        rows = dot(pick, block, dims)
        return jnp.where(own_lanes, rows, 0.0).astype(BF16)

    far_qk = dot(far(q_ref[:, half]), fold0) + dot(far(k_ref[:, half]), fold1)
    far_vo = dot(far(v_ref[:, half]), fold0) + dot(far(d_attn[HALF:], NT), fold1)
    b_send[...] = jnp.concatenate(
        [far_qk.reshape(8, 8, ROWS), far_vo.reshape(8, 8, ROWS)], axis=1
    ).astype(BF16)

    pl.semaphore_wait(barrier, 17 + jnp.where(is_owner, 70, 8))

    def b_copy(j):
        return pltpu.make_async_remote_copy(
            src_ref=b_send.at[j], dst_ref=b_recv.at[seq], send_sem=b_ss.at[j], recv_sem=b_rs,
            device_id=(owner_of(j), x), device_id_type=MESH,
        )

    def b_start(j, carry):
        @pl.when(owner_of(j) != seq)
        def _():
            b_copy(j).start()
        return carry

    lax.fori_loop(0, 8, b_start, 0)

    @pl.when(is_owner)
    def _():
        pltpu.make_async_copy(b_send.at[z], b_recv.at[seq], b_rs).start()

    a_copies = []
    for r in range(1, 4):
        d = (pos + r) % 4
        a_copies.append(
            send(a_send.at[d], a_recv.at[pos], a_ss.at[r - 1], a_rs.at[r - 1], (first + d, x))
        )
    for copy in a_copies:
        copy.wait_recv()

    at = first * ROWS
    key_ok = at + iota((SEG, 1), 0) < kept
    row_ok = jnp.where(at + iota((1, SEG), 1) < kept, 1.0, 0.0)
    for h in range(2):
        parts = [
            jnp.concatenate(
                [a_recv[s, 96 * t + HD * h : 96 * t + HD * h + HD, :] for s in range(4)], axis=1
            )
            for t in range(4)
        ]
        outs = head_pass(*parts, key_ok, row_ok)
        for t in range(4):
            for d in range(4):
                a_back[d, 96 * t + HD * h : 96 * t + HD * h + HD, :] = outs[t][
                    :, ROWS * d : ROWS * d + ROWS
                ]
    a_ret[pos] = a_back[pos]
    for r in range(1, 4):
        d = (pos + r) % 4
        a_copies.append(
            send(a_back.at[d], a_ret.at[pos], ar_ss.at[r - 1], ar_rs.at[r - 1], (first + d, x))
        )

    def back_copy(s):
        return pltpu.make_async_remote_copy(
            src_ref=b_back.at[s], dst_ref=b_ret.at[z], send_sem=br_ss, recv_sem=br_rs,
            device_id=(s, x), device_id_type=MESH,
        )

    @pl.when(is_owner)
    def _():
        pltpu.make_async_copy(b_recv, b_recv, b_rs).wait()
        rows = b_recv[...].astype(F32)
        qk = turn(rows[:, :8, :].reshape(SEG, ROWS))
        vo = turn(rows[:, 8:, :].reshape(SEG, ROWS))
        key_ok = 16 * iota((SEG, 1), 0) + z < kept
        row_ok = jnp.where(16 * iota((1, SEG), 1) + z < kept, 1.0, 0.0)
        outs = head_pass(
            qk[:HD], qk[HD : 2 * HD], vo[:HD], vo[HD : 2 * HD], key_ok, row_ok
        )
        pad = jnp.zeros((ROWS - 2 * HD, SEG), F32)
        packs = [
            jnp.transpose(
                jnp.concatenate([outs[t].astype(F32), outs[t + 1].astype(F32), pad], axis=0)
            ).reshape(64, 8, ROWS)
            for t in (0, 2)
        ]
        b_back[...] = jnp.concatenate(packs, axis=1).astype(BF16)

        def back(r, carry):
            back_copy((seq + r) % 64).start()
            return carry

        lax.fori_loop(1, 64, back, 0)
        pltpu.make_async_copy(b_back.at[seq], b_ret.at[z], br_rs).start()

    for copy in a_copies[3:]:
        copy.wait_recv()
    near_out = [
        jnp.concatenate([a_ret[s, 96 * t : 96 * t + 96, :] for s in range(4)], axis=0)
        for t in range(4)
    ]
    part[:HALF, :] = dot(near_out[0], grad)
    for t, ref in ((1, dq_ref), (2, dk_ref), (3, dv_ref)):
        ref[:, :HALF] = turn(near_out[t])

    pltpu.make_async_copy(b_ret, b_ret, br_rs).wait()
    rows = b_ret[...].astype(F32)
    back_ad = rows[:, :8, :].reshape(64, ROWS).astype(BF16)
    back_kv = rows[:, 8:, :].reshape(64, ROWS).astype(BF16)
    t_in = iota((HALF, 64), 0) - HD * (iota((HALF, 64), 1) >> 3)
    own_rows = (t_in >= 0) & (t_in < HD)
    r64 = iota((ROWS, 64), 1)
    place = one_hot(iota((ROWS, 64), 0) == 16 * (r64 & 7) + (r64 >> 3))
    attn_far = jnp.where(own_rows, dot(fold0, back_ad, NT), 0.0).astype(BF16)
    part[HALF:, :] = dot(attn_far, dot(pick, grad).astype(BF16))

    def spread(block, fold):
        rows = jnp.where(own_lanes, dot(block, fold, NT), 0.0).astype(BF16)
        return dot(place, rows).astype(BF16)

    dq_ref[:, half] = spread(back_ad, fold1)
    dk_ref[:, half] = spread(back_kv, fold0)
    dv_ref[:, half] = spread(back_kv, fold1)

    there = pl.multiple_of((1 - core) * HALF, HALF)
    here = pl.multiple_of(core * HALF, HALF)
    c_send[...] = part[pl.ds(there, HALF), :].astype(BF16)
    c_copy = send(c_send, c_recv, c_ss, c_rs, partner)
    c_copy.wait_recv()
    total = part[pl.ds(here, HALF), :] + c_recv[...].astype(F32)
    for i in range(2):
        block = total[:, HALF * i : HALF * i + HALF].reshape(4, 96, HALF)
        h_ref[i] = block
        s1_send[i] = block.astype(BF16)
    own = (x, y)
    peers = (x_peer, y_peer)

    copies = [c_copy]
    step = []
    for r in range(1, 4):
        for i in range(2):
            step.append(
                send(
                    s1_send.at[i, (own[i] + r) % 4], s1_recv.at[i, r - 1],
                    s1_ss.at[i, r - 1], s1_rs.at[i, r - 1], peers[i](r),
                )
            )
    for copy in step:
        copy.wait_recv()
    copies += step
    for i in range(2):
        block = h_ref[i, own[i]]
        for r in range(3):
            block += s1_recv[i, r].astype(F32)
        block = block.reshape(4, 24, HALF)
        s2_own[i] = block
        s2_send[i] = block.astype(BF16)
    step = []
    for r in range(1, 4):
        for i in range(2):
            step.append(
                send(
                    s2_send.at[i, (own[1 - i] + r) % 4], s2_recv.at[i, r - 1],
                    s2_ss.at[i, r - 1], s2_rs.at[i, r - 1], peers[1 - i](r),
                )
            )
    for copy in step:
        copy.wait_recv()
    copies += step
    for i in range(2):
        block = s2_own[i, own[1 - i]]
        for r in range(3):
            block += s2_recv[i, r].astype(F32)
        z_buf[z, i] = block.astype(BF16)
    step = []
    for r in range(1, 8):
        step.append(send(z_buf.at[z], z_buf.at[z], z_ss.at[r - 1], z_rs.at[r - 1], z_peer(r)))
    for copy in step:
        copy.wait_recv()
    copies += step
    scale = (32768.0) ** -0.5
    for i in range(2):
        block = z_buf[0, i].astype(F32)
        for r in range(1, 8):
            block += z_buf[r, i].astype(F32)
        g1[i, own[1 - i]] = (block * scale).astype(BF16)
    step = []
    for r in range(1, 4):
        for i in range(2):
            piece = g1.at[i, own[1 - i]]
            step.append(
                send(piece, piece, g1_ss.at[i, r - 1], g1_rs.at[i, r - 1], peers[1 - i](r))
            )
    for copy in step:
        copy.wait_recv()
    copies += step
    for i in range(2):
        g2[i, own[i]] = g1[i]
    step = []
    for r in range(1, 4):
        for i in range(2):
            step.append(
                send(
                    g1.at[i], g2.at[i, own[i]],
                    g2_ss.at[i, r - 1], g2_rs.at[i, r - 1], peers[i](r),
                )
            )
    for copy in step:
        copy.wait_recv()
    copies += step
    last = send(g2, g3, g3_ss, g3_rs, partner)
    copies.append(last)
    for i in range(2):
        dw_ref[pl.ds(here, HALF), HALF * i : HALF * i + HALF] = (
            g2[i].astype(F32).reshape(HALF, HALF)
        )
    last.wait_recv()
    for i in range(2):
        dw_ref[pl.ds(there, HALF), HALF * i : HALF * i + HALF] = (
            g3[i].astype(F32).reshape(HALF, HALF)
        )

    for copy in a_copies + copies:
        copy.wait_send()

    def b_done(j, carry):
        @pl.when(owner_of(j) != seq)
        def _():
            b_copy(j).wait_send()
        return carry

    lax.fori_loop(0, 8, b_done, 0)

    @pl.when(is_owner)
    def _():
        part_of = b_back.at[pl.ds(0, 63)]
        pltpu.make_async_remote_copy(
            src_ref=part_of, dst_ref=part_of, send_sem=br_ss, recv_sem=br_rs,
            device_id=partner, device_id_type=MESH,
        ).wait_send()


def per_device(queries, keys, values, grad_out, w_out, kept_tiles):
    vmem = pl.BlockSpec(memory_space=pltpu.VMEM)
    dma = pltpu.SemaphoreType.DMA
    block = jax.ShapeDtypeStruct((ROWS, WIDTH), BF16)
    outs = pl.pallas_call(
        kernel,
        out_shape=(block, block, block, jax.ShapeDtypeStruct((WIDTH, WIDTH), F32)),
        in_specs=[pl.BlockSpec(memory_space=pltpu.SMEM)] + [vmem] * 5,
        out_specs=(vmem,) * 4,
        scratch_shapes=[
            pltpu.VMEM((4, HALF, ROWS), BF16),
            pltpu.VMEM((4, HALF, ROWS), BF16),
            pltpu.VMEM((4, HALF, ROWS), BF16),
            pltpu.VMEM((4, HALF, ROWS), BF16),
            pltpu.VMEM((8, 16, ROWS), BF16),
            pltpu.VMEM((64, 16, ROWS), BF16),
            pltpu.VMEM((64, 16, ROWS), BF16),
            pltpu.VMEM((8, 16, ROWS), BF16),
            pltpu.VMEM((WIDTH, WIDTH), F32),
            pltpu.VMEM((HALF, WIDTH), BF16),
            pltpu.VMEM((HALF, WIDTH), BF16),
            pltpu.VMEM((2, 4, 96, HALF), F32),
            pltpu.VMEM((2, 4, 96, HALF), BF16),
            pltpu.VMEM((2, 3, 96, HALF), BF16),
            pltpu.VMEM((2, 4, 24, HALF), F32),
            pltpu.VMEM((2, 4, 24, HALF), BF16),
            pltpu.VMEM((2, 3, 24, HALF), BF16),
            pltpu.VMEM((8, 2, 24, HALF), BF16),
            pltpu.VMEM((2, 4, 24, HALF), BF16),
            pltpu.VMEM((2, 4, 4, 24, HALF), BF16),
            pltpu.VMEM((2, 4, 4, 24, HALF), BF16),
            dma((3,)), dma((3,)), dma((3,)), dma((3,)),
            dma((8,)), dma, dma, dma, dma, dma,
            dma((2, 3)), dma((2, 3)), dma((2, 3)), dma((2, 3)), dma((7,)), dma((7,)),
            dma((2, 3)), dma((2, 3)), dma((2, 3)), dma((2, 3)), dma, dma,
        ],
        compiler_params=pltpu.CompilerParams(
            collective_id=0, has_side_effects=True, vmem_limit_bytes=56 * 1024 * 1024
        ),
        name="grouped_attention_grads",
    )(kept_tiles, queries[0], keys[0], values[0], grad_out[0], w_out)
    return (outs[0][None], outs[1][None], outs[2][None], outs[3])


def solution(mesh):
    rows = P("slide", "seq", None)
    return jax.shard_map(
        per_device,
        mesh=mesh,
        in_specs=(rows, rows, rows, rows, P(), P("slide")),
        out_specs=(rows, rows, rows, P()),
        check_vma=False,
    )
```

time: 604 us -> 74.5 us (0.12)
  blocking collectives: 277 us -> 0 us
  waiting for transfers between devices: 258 us -> 0 us
  Pallas kernels: 0 us -> 64.9 us
  matrix products: 18.6 us -> 0 us
  between operations: 15.5 us -> 1.29 us
  other arithmetic: 10.7 us -> 0 us
  local copies, waits for them, and re-layouts: 17.4 us -> 8.07 us
    all_gather x6 -> x0, blocking collectives: 277 us -> none  [the longest x1 50.6 us: per_device(): lax.all_gather(far_grads.reshape(selected_row_index, half_width), 'seq',...]
    psum x1 -> x0, waiting for transfers between devices: 236 us -> none  [per_device(): weight_sum = lax.psum(weight_term, ('seq', 'slide'))]
    pallas_call x0 -> x1, Pallas kernels: none -> 64.9 us  [per_device(): pl.pallas_call(kernel, out_shape=(block, block, block, jax.ShapeDtypeStru...]
    ppermute x4 -> x0, waiting for transfers between devices: 21.3 us -> none  [from_partner(): return lax.ppermute(block, axis, route)]
    dot_general x32 -> x0, matrix products: 18.6 us -> none  [the longest x5 3.85 us: head_pass(): jnp.einsum('hqk,khd->qhd', d_scores, key_rows, preferred_element_type=jnp...]
    concatenate x11 -> x0, other arithmetic: 7.36 us -> none  [the longest x2 1.94 us: per_device(): keys_values = jnp.concatenate([keys_values, received], axis=0)]
  transfers between devices with their start and end apart: 5 -> 0, of which waited for: 4 -> 0; matrix products, arithmetic and copies ran while one was open for 3% -> 0% of each run, Pallas kernels for 0% -> 0%
where the time goes in v1:
time: 74.5 us; the launch traced here: 74.3 us
  Pallas kernels  64.9 us (87%)
  local copies, waits for them, and re-layouts  8.07 us (11%)
  between operations  1.29 us (2%)
    pallas_call x1, Pallas kernels, per_device(): pl.pallas_call(kernel, out_shape=(block, block, block, jax.ShapeDtypeStru...  64.9 us
    unnamed x4, local copies, waits for them, and re-layouts  8.07 us

profile of v1, /device:TPU:1, one launch (start us, length us, event | category | flops | bytes accessed | tf_op | source)
XLA Modules:
  0.0 74.3 jit_solution(10219013841074141661)
XLA Ops:
  1.3 64.9 %grouped_attention_grads.1 = (bf16[128,768]{1,0:T(8,128)(2,1)}, bf16[128,768]{1,0:T(8,128)(2,1)}, bf16[128,768]{1,0:T(8,128)(2,1)}, f32[768,768]{1,0:T(8,128)}) custom-call(s32[1]{0:T(128)S(6)} %copy.14.kept_ref, bf16[128,768]{1,0:T(8,128)(2,1)} %bitcast.7, bf16[128,768]{1,0:T(8,128)(2,1)} %bitcast.8, bf16[128,768]{1,0:T(8,128)(2,1)} %bitcast.9, ...), custom_call_target="tpu_custom_call" | custom-call | tf_op jit(solution)/shard_map/grouped_attention_grads/pallas_call | solution.py:391
  66.2 1.6 %copy.15 = bf16[1,128,768]{2,1,0:T(8,128)(2,1)} copy(bf16[1,128,768]{2,1,0:T(8,128)(2,1)} %bitcast.13) | data formatting | bytes 393216
  67.8 1.6 %copy.16 = bf16[1,128,768]{2,1,0:T(8,128)(2,1)} copy(bf16[1,128,768]{2,1,0:T(8,128)(2,1)} %bitcast.12) | data formatting | bytes 393216
  69.4 1.6 %copy.17 = bf16[1,128,768]{2,1,0:T(8,128)(2,1)} copy(bf16[1,128,768]{2,1,0:T(8,128)(2,1)} %bitcast.11) | data formatting | bytes 393216
  71.0 3.2 %copy.18 = f32[768,768]{1,0:T(8,128)} copy(f32[768,768]{1,0:T(8,128)} %get-tuple-element.19) | data formatting | bytes 4718592

commit v2 on v1

v2 whole, which is shorter than its diff:
```python
import jax
import jax.numpy as jnp
from jax import lax
from jax.experimental import pallas as pl
from jax.experimental.pallas import tpu as pltpu
from jax.sharding import PartitionSpec as P

ROWS = 128
WIDTH = 768
HALF = 384
HD = 48
SEG = 512
PART = (24, HALF)
F32 = jnp.float32
BF16 = jnp.bfloat16
MESH = pl.DeviceIdType.MESH
NN = (((1,), (0,)), ((), ()))
NT = (((1,), (1,)), ((), ()))
SCALING = HD ** -0.5


def dot(a, b, dims=NN):
    return lax.dot_general(a, b, dims, preferred_element_type=F32)


def iota(shape, dim):
    return lax.broadcasted_iota(jnp.int32, shape, dim)


def one_hot(mask):
    return jnp.where(mask, 1.0, 0.0).astype(BF16)


def turn(a):
    return jnp.transpose(a.astype(F32)).astype(BF16)


def softmax(scores, key_ok):
    scores = jnp.where(key_ok, scores * SCALING, -1e30)
    grown = jnp.exp(scores - jnp.max(scores, axis=0, keepdims=True))
    return grown * (1.0 / jnp.sum(grown, axis=0, keepdims=True))


def kernel(
    kept_ref, q_ref, k_ref, v_ref, g_ref, w_ref,
    dq_ref, dk_ref, dv_ref, dw_ref,
    a_send, a_recv, a_back, a_ret, g_all, probs_ref, low_ref,
    b_send, b_recv, kv_all, dkv_send, dkv_recv, b_back, b_ret,
    pa_own, pa_send, pa_recv, pb_own, pb_send, pb_recv, za, tb, g1, g2, g3,
    a_ss, a_rs, ar_ss, ar_rs, gr_ss, gr_rs, b_ss, b_rs, kv_ss, kv_rs, dkv_ss, dkv_rs,
    br_ss, br_rs, pa_ss, pa_rs, pb_ss, pb_rs, za_ss, za_rs, tb_ss, tb_rs,
    g1a_ss, g1a_rs, g1b_ss, g1b_rs, g2_ss, g2_rs, g3_ss, g3_rs,
):
    seq = lax.axis_index("seq")
    x = lax.axis_index("slide")
    core = seq % 2
    y = (seq // 2) % 4
    z = seq // 8
    pos = seq % 4
    tee = seq % 8
    first = seq - pos
    m = y // 2

    def x_peer(r):
        return (seq, (x + r) % 4)

    def y_peer(r):
        return ((z * 4 + (y + r) % 4) * 2 + core, x)

    def z_peer(r):
        return (((z + r) % 8) * 8 + tee, x)

    def plane_peer(r):
        return (z * 8 + (tee + r) % 8, x)

    def xm_peer(rx, rm):
        return ((z * 4 + (y + 2 * rm) % 4) * 2 + core, (x + rx) % 4)

    partner = (seq + 1 - 2 * core, x)
    across = (first + (pos + 2) % 4, x)

    started = []

    def send(src, dst, ss, rs, device):
        copy = pltpu.make_async_remote_copy(
            src_ref=src, dst_ref=dst, send_sem=ss, recv_sem=rs,
            device_id=device, device_id_type=MESH,
        )
        copy.start()
        started.append(copy)
        return copy

    def arrived(copies):
        for copy in copies:
            copy.wait_recv()

    barrier = pltpu.get_barrier_semaphore()

    def greet(device):
        pl.semaphore_signal(barrier, inc=1, device_id=device, device_id_type=MESH)

    for r in range(1, 8):
        greet(z_peer(r))
    for r in range(1, 8):
        greet(plane_peer(r))
    for rx in range(1, 4):
        for rm in range(2):
            greet(xm_peer(rx, rm))

    kept = kept_ref[0]
    far = pl.ds(HALF, HALF)
    col_ok = jnp.where(seq * ROWS + iota((1, ROWS), 1) < kept, 1.0, 0.0)
    grad = g_ref[...]
    d_attn = (dot(w_ref[...], grad, NT) * col_ok).astype(BF16)
    near = (turn(q_ref[:, :HALF]), turn(k_ref[:, :HALF]), turn(v_ref[:, :HALF]), d_attn[:HALF])
    for d in range(4):
        for t in range(4):
            a_send[d, 96 * t : 96 * t + 96, :] = near[t][96 * d : 96 * d + 96]
    a_recv[pos] = a_send[pos]
    g_all[pos] = grad

    r64 = iota((64, ROWS), 0)
    pick = one_hot(iota((64, ROWS), 1) == 16 * (r64 & 7) + (r64 >> 3))
    l_in = iota((64, HALF), 1) - HD * (iota((64, HALF), 0) >> 3)
    own_lanes = (l_in >= 0) & (l_in < HD)
    feat = iota((HALF, ROWS), 0)
    feat = feat - HD * ((feat * 683) >> 15)
    lane = iota((HALF, ROWS), 1)
    fold0 = one_hot(lane == feat)
    fold1 = one_hot(lane == feat + HD)

    def dilated(block, dims=NN):
        rows = dot(pick, block, dims)
        return jnp.where(own_lanes, rows, 0.0).astype(BF16)

    def tops(block):
        return block.reshape(8, 8, block.shape[-1])

    far_ko = dot(dilated(k_ref[:, far]), fold0) + dot(dilated(d_attn[HALF:], NT), fold1)
    far_qv = dot(dilated(q_ref[:, far]), fold0) + dot(dilated(v_ref[:, far]), fold1)
    far_g = dot(pick, grad)
    b_send[:, :, :ROWS] = jnp.concatenate([tops(far_ko), tops(far_qv)], axis=1).astype(BF16)
    b_send[:, :, ROWS:] = jnp.concatenate(
        [tops(far_g[:, :HALF]), tops(far_g[:, HALF:])], axis=1
    ).astype(BF16)
    b_recv[z] = b_send[z]

    pl.semaphore_wait(barrier, 20)

    b_in = [
        send(b_send.at[(z + r) % 8], b_recv.at[z], b_ss.at[r - 1], b_rs.at[r - 1], z_peer(r))
        for r in (4, 3, 5, 2, 6, 1, 7)
    ]
    a_in = [
        send(
            a_send.at[(pos + r) % 4], a_recv.at[pos],
            a_ss.at[r - 1], a_rs.at[r - 1], (first + (pos + r) % 4, x),
        )
        for r in range(1, 4)
    ]
    g_across = send(g_ref, g_all.at[pos], gr_ss.at[0], gr_rs.at[0], across)
    g_near = send(g_ref, g_all.at[pos], gr_ss.at[1], gr_rs.at[1], partner)

    arrived(b_in)
    rows = b_recv[:, :, :ROWS].astype(F32)
    ko = rows[:, :8, :].reshape(64, ROWS)
    qv = rows[:, 8:, :].reshape(64, ROWS)
    lane64 = iota((64, ROWS), 1)
    left = lane64 < HD
    right = (lane64 >= HD) & (lane64 < 2 * HD)
    kv_all[tee] = jnp.where(left, ko, jnp.where(right, qv, 0.0)).astype(BF16)
    kv_in = [
        send(kv_all.at[tee], kv_all.at[tee], kv_ss.at[r - 1], kv_rs.at[r - 1], plane_peer(r))
        for r in range(1, 8)
    ]
    q_rows = jnp.where(left, qv, 0.0).astype(BF16)
    o_rows = jnp.where(right, ko, 0.0).astype(BF16)
    q_cols = turn(q_rows)
    o_cols = turn(o_rows)

    arrived(a_in)
    at = first * ROWS
    key_ok = at + iota((SEG, 1), 0) < kept
    row_ok = jnp.where(at + iota((1, SEG), 1) < kept, 1.0, 0.0)

    def head_rows(t, h):
        lo = 96 * t + HD * h
        return jnp.concatenate([a_recv[s, lo : lo + HD, :] for s in range(4)], axis=1)

    attn_near = []
    for h in range(2):
        probs = softmax(dot(turn(head_rows(1, h)), head_rows(0, h)), key_ok)
        low = probs.astype(BF16)
        probs_ref[h] = probs
        low_ref[h] = low
        attn_near.append((dot(head_rows(2, h), low) * row_ok).astype(BF16))

    arrived([g_across])
    g_fwd = send(
        g_all.at[(pos + 2) % 4], g_all.at[(pos + 2) % 4], gr_ss.at[2], gr_rs.at[2], partner
    )

    arrived(kv_in)
    kv = kv_all[...].reshape(SEG, ROWS)
    kv_cols = turn(kv)
    r512 = iota((SEG, 1), 0)
    far_key_ok = (
        (((r512 >> 3) & 7) * 8 + (r512 >> 6)) * ROWS + 16 * (r512 & 7) + z < kept
    )
    c64 = iota((1, 64), 1)
    far_row_ok = jnp.where(((c64 >> 3) * 8 + tee) * ROWS + 16 * (c64 & 7) + z < kept, 1.0, 0.0)
    far_probs = softmax(dot(kv, q_cols), far_key_ok)
    far_low = far_probs.astype(BF16)
    attn_far = (dot(kv_cols, far_low) * far_row_ok).astype(BF16)
    g_rows = b_recv[:, :, ROWS:].astype(F32)
    for i in range(2):
        block = dot(
            attn_far[HD : 2 * HD], g_rows[:, 8 * i : 8 * i + 8, :].reshape(64, HALF).astype(BF16)
        )
        for half in range(2):
            piece = block[24 * half : 24 * half + 24]
            pb_own[2 * half + i] = piece
            pb_send[2 * half + i] = piece.astype(BF16)
    pb_in = [
        send(pb_send.at[(x + r) % 4], pb_recv.at[r - 1], pb_ss.at[r - 1], pb_rs.at[r - 1], x_peer(r))
        for r in range(1, 4)
    ]

    arrived([g_near, g_fwd])
    attn = jnp.concatenate(attn_near, axis=0)
    block = dot(attn, g_all[...].reshape(SEG, WIDTH))
    for i in range(4):
        for j in range(2):
            piece = block[24 * i : 24 * i + 24, HALF * j : HALF * j + HALF]
            pa_own[i, j] = piece
            pa_send[i, j] = piece.astype(BF16)
    pa_in = [
        send(
            pa_send.at[(x + rx) % 4, (m + rm) % 2], pa_recv.at[2 * rx + rm - 1],
            pa_ss.at[2 * rx + rm - 1], pa_rs.at[2 * rx + rm - 1], xm_peer(rx, rm),
        )
        for rx, rm in ((2, 1), (1, 1), (3, 1), (2, 0), (1, 0), (3, 0), (0, 1))
    ]

    row_dot = jnp.sum(o_cols.astype(F32) * attn_far.astype(F32), axis=0, keepdims=True)
    far_ds = (far_probs * (dot(kv, o_cols) - row_dot)).astype(BF16)
    far_dq = jnp.transpose(dot(kv_cols, far_ds) * SCALING)
    dkv = dot(far_ds, q_rows) * SCALING + dot(far_low, o_rows)
    dkv = dkv.reshape(8, 64, ROWS)
    dkv_send[...] = dkv.astype(BF16)
    dkv_recv[tee] = dkv_send[tee]
    dkv_in = [
        send(
            dkv_send.at[(tee + r) % 8], dkv_recv.at[tee],
            dkv_ss.at[r - 1], dkv_rs.at[r - 1], plane_peer(r),
        )
        for r in range(1, 8)
    ]

    arrived(pb_in)
    piece = pb_own[x]
    for r in range(3):
        piece += pb_recv[r].astype(F32)
    tb[tee] = piece.astype(BF16)
    tb_in = [
        send(tb.at[tee], tb.at[tee], tb_ss.at[r - 1], tb_rs.at[r - 1], plane_peer(r))
        for r in range(1, 8)
    ]

    def near_back(h):
        q_t, k_t, v_t, o_t = (head_rows(t, h) for t in range(4))
        row_dot = jnp.sum(o_t.astype(F32) * attn_near[h].astype(F32), axis=0, keepdims=True)
        d_scores = (probs_ref[h] * (dot(turn(v_t), o_t) - row_dot)).astype(BF16)
        outs = (
            dot(k_t, d_scores) * SCALING,
            dot(q_t, d_scores, NT) * SCALING,
            dot(o_t, low_ref[h], NT),
        )
        for t in range(3):
            lo = 96 * t + HD * h
            for d in range(4):
                a_back[d, lo : lo + HD, :] = outs[t][:, ROWS * d : ROWS * d + ROWS].astype(BF16)

    near_back(0)
    arrived(pa_in)
    piece = pa_own[x, m]
    for r in range(7):
        piece += pa_recv[r].astype(F32)
    za[z] = piece.astype(BF16)
    za_in = [
        send(za.at[z], za.at[z], za_ss.at[r - 1], za_rs.at[r - 1], z_peer(r))
        for r in (4, 3, 5, 2, 6, 1, 7)
    ]
    near_back(1)
    a_ret[pos] = a_back[pos]
    ar_in = [
        send(
            a_back.at[(pos + r) % 4], a_ret.at[pos],
            ar_ss.at[r - 1], ar_rs.at[r - 1], (first + (pos + r) % 4, x),
        )
        for r in range(1, 4)
    ]

    arrived(dkv_in)
    dkv = dkv_recv[0].astype(F32)
    for r in range(1, 8):
        dkv += dkv_recv[r].astype(F32)
    b_back[...] = jnp.concatenate([tops(far_dq), tops(dkv)], axis=1).astype(BF16)
    b_ret[z] = b_back[z]
    br_in = [
        send(b_back.at[(z + r) % 8], b_ret.at[z], br_ss.at[r - 1], br_rs.at[r - 1], z_peer(r))
        for r in range(1, 8)
    ]

    scale = 32768.0 ** -0.5
    mine = z % 2 == core

    def total(ref):
        piece = ref[0].astype(F32)
        for r in range(1, 8):
            piece += ref[r].astype(F32)
        return (piece * scale).astype(BF16)

    def g1b_copy(r):
        slot = g1.at[1, z // 2]
        return pltpu.make_async_remote_copy(
            src_ref=slot, dst_ref=slot, send_sem=g1b_ss.at[r - 1], recv_sem=g1b_rs.at[r - 1],
            device_id=z_peer(r), device_id_type=MESH,
        )

    arrived(tb_in)
    tb_total = total(tb)

    @pl.when(mine)
    def _():
        g1[1, z // 2] = tb_total
        for r in (4, 3, 5, 2, 6, 1, 7):
            g1b_copy(r).start()

    arrived(za_in)
    g1[0, x] = total(za)
    g1a_in = [
        send(g1.at[0, x], g1.at[0, x], g1a_ss.at[r - 1], g1a_rs.at[r - 1], x_peer(r))
        for r in (2, 1, 3)
    ]

    arrived(ar_in)
    for t, ref in ((0, dq_ref), (1, dk_ref), (2, dv_ref)):
        ref[:, :HALF] = turn(
            jnp.concatenate([a_ret[s, 96 * t : 96 * t + 96, :] for s in range(4)], axis=0)
        )

    own = (y, x)

    def g2_sends(i, peer):
        copies = [
            send(g1.at[i], g2.at[i, own[i]], g2_ss.at[i, r - 1], g2_rs.at[i, r - 1], peer(r))
            for r in (2, 1, 3)
        ]
        send(g1.at[i], g3.at[i, own[i]], g3_ss.at[i, 0], g3_rs.at[i, 0], partner)
        g2[i, own[i]] = g1[i]
        return copies

    arrived(g1a_in)
    g2a_in = g2_sends(0, y_peer)

    @pl.when(mine)
    def _():
        for r in (2, 4, 6):
            g1b_copy(r).wait_recv()

    @pl.when(jnp.logical_not(mine))
    def _():
        for r in (1, 3, 5, 7):
            g1b_copy(r).wait_recv()

    g2b_in = g2_sends(1, x_peer)

    arrived(br_in)
    rows = b_ret[...].astype(F32)
    back_q = rows[:, :8, :].reshape(64, ROWS).astype(BF16)
    back_kv = rows[:, 8:, :].reshape(64, ROWS).astype(BF16)
    r64 = iota((ROWS, 64), 1)
    place = one_hot(iota((ROWS, 64), 0) == 16 * (r64 & 7) + (r64 >> 3))

    def spread(block, fold):
        rows = jnp.where(own_lanes, dot(block, fold, NT), 0.0).astype(BF16)
        return dot(place, rows).astype(BF16)

    dq_ref[:, far] = spread(back_q, fold0)
    dk_ref[:, far] = spread(back_kv, fold0)
    dv_ref[:, far] = spread(back_kv, fold1)

    for j, r in enumerate((2, 1, 3)):
        for i, copies in ((0, g2a_in), (1, g2b_in)):
            arrived([copies[j]])
            slot = (own[i] + 4 - r) % 4
            send(g2.at[i, slot], g3.at[i, slot], g3_ss.at[i, r], g3_rs.at[i, r], partner)

    def put(ref, c):
        for s in range(4):
            at = pl.multiple_of(96 * ((s % 2) * 2 + c), 96)
            dw_ref[pl.ds(at, 96), HALF * (s // 2) : HALF * (s // 2) + HALF] = (
                ref[0, s].astype(F32).reshape(96, HALF)
            )
            for k in range(4):
                at = pl.multiple_of(HALF + HD * (2 * k + c) + 24 * (s // 2), 8)
                dw_ref[pl.ds(at, 24), HALF * (s % 2) : HALF * (s % 2) + HALF] = (
                    ref[1, s, k].astype(F32)
                )

    put(g2, core)
    for i in range(2):
        for r in range(4):
            pltpu.make_async_copy(g3.at[i, 0], g3.at[i, 0], g3_rs.at[i, r]).wait()
    put(g3, 1 - core)

    for copy in started:
        copy.wait_send()

    @pl.when(mine)
    def _():
        for r in range(1, 8):
            g1b_copy(r).wait_send()


def pass_on(*refs):
    ins, outs, held, in_sem, out_sem = refs[:4], refs[4:8], refs[8:12], refs[12], refs[13]
    chunks = [(i, slice(None)) for i in range(3)]
    chunks += [(3, pl.ds(192 * j, 192)) for j in range(4)]
    arriving = []
    for n, (i, at) in enumerate(chunks):
        arriving.append(
            pltpu.make_async_copy(ins[i].at[at], held[i].at[at], in_sem.at[n])
        )
        arriving[-1].start()
    leaving = []
    for n, (i, at) in enumerate(chunks):
        arriving[n].wait()
        leaving.append(
            pltpu.make_async_copy(held[i].at[at], outs[i].at[at], out_sem.at[n])
        )
        leaving[-1].start()
    for copy in leaving:
        copy.wait()


def per_device(queries, keys, values, grad_out, w_out, kept_tiles):
    vmem = pl.BlockSpec(memory_space=pltpu.VMEM)
    anywhere = pl.BlockSpec(memory_space=pl.ANY)
    dma = pltpu.SemaphoreType.DMA
    block = jax.ShapeDtypeStruct((ROWS, WIDTH), BF16)
    out_shape = (block, block, block, jax.ShapeDtypeStruct((WIDTH, WIDTH), F32))
    outs = pl.pallas_call(
        kernel,
        out_shape=out_shape,
        in_specs=[pl.BlockSpec(memory_space=pltpu.SMEM)] + [vmem] * 5,
        out_specs=(vmem,) * 4,
        scratch_shapes=[
            pltpu.VMEM((4, HALF, ROWS), BF16),
            pltpu.VMEM((4, HALF, ROWS), BF16),
            pltpu.VMEM((4, 288, ROWS), BF16),
            pltpu.VMEM((4, 288, ROWS), BF16),
            pltpu.VMEM((4, ROWS, WIDTH), BF16),
            pltpu.VMEM((2, SEG, SEG), F32),
            pltpu.VMEM((2, SEG, SEG), BF16),
            pltpu.VMEM((8, 16, SEG), BF16),
            pltpu.VMEM((8, 16, SEG), BF16),
            pltpu.VMEM((8, 64, ROWS), BF16),
            pltpu.VMEM((8, 64, ROWS), BF16),
            pltpu.VMEM((8, 64, ROWS), BF16),
            pltpu.VMEM((8, 16, ROWS), BF16),
            pltpu.VMEM((8, 16, ROWS), BF16),
            pltpu.VMEM((4, 2) + PART, F32),
            pltpu.VMEM((4, 2) + PART, BF16),
            pltpu.VMEM((7,) + PART, BF16),
            pltpu.VMEM((4,) + PART, F32),
            pltpu.VMEM((4,) + PART, BF16),
            pltpu.VMEM((3,) + PART, BF16),
            pltpu.VMEM((8,) + PART, BF16),
            pltpu.VMEM((8,) + PART, BF16),
            pltpu.VMEM((2, 4) + PART, BF16),
            pltpu.VMEM((2, 4, 4) + PART, BF16),
            pltpu.VMEM((2, 4, 4) + PART, BF16),
            dma((3,)), dma((3,)), dma((3,)), dma((3,)), dma((3,)), dma((3,)),
            dma((7,)), dma((7,)), dma((7,)), dma((7,)), dma((7,)), dma((7,)),
            dma((7,)), dma((7,)), dma((7,)), dma((7,)), dma((3,)), dma((3,)),
            dma((7,)), dma((7,)), dma((7,)), dma((7,)),
            dma((3,)), dma((3,)), dma((7,)), dma((7,)), dma((2, 3)), dma((2, 3)),
            dma((2, 4)), dma((2, 4)),
        ],
        compiler_params=pltpu.CompilerParams(
            collective_id=0, has_side_effects=True, vmem_limit_bytes=56 * 1024 * 1024
        ),
        name="grouped_attention_grads",
    )(kept_tiles, queries[0], keys[0], values[0], grad_out[0], w_out)
    outs = pl.pallas_call(
        pass_on,
        out_shape=out_shape,
        in_specs=[anywhere] * 4,
        out_specs=(anywhere,) * 4,
        scratch_shapes=[pltpu.VMEM(s.shape, s.dtype) for s in out_shape]
        + [dma((7,)), dma((7,))],
        name="pass_on",
    )(*outs)
    return (outs[0][None], outs[1][None], outs[2][None], outs[3])


def solution(mesh):
    rows = P("slide", "seq", None)
    return jax.shard_map(
        per_device,
        mesh=mesh,
        in_specs=(rows, rows, rows, rows, P(), P("slide")),
        out_specs=(rows, rows, rows, P()),
        check_vma=False,
    )
```

time: 74.5 us -> 53.7 us (0.72)
  Pallas kernels: 64.9 us -> 52.2 us
  local copies, waits for them, and re-layouts: 8.07 us -> 0 us
    pallas_call x1 -> x2, Pallas kernels: 64.9 us -> 52.2 us  [the longest x1 49.3 us: per_device(): pl.pallas_call(kernel, out_shape=out_shape, in_specs=[pl.BlockSpec(memory...]
    unnamed x4 -> x0, local copies, waits for them, and re-layouts: 8.07 us -> none
where the time goes in v2:
time: 53.7 us; the launch traced here: 53.5 us
  Pallas kernels  52.2 us (97%)
  between operations  1.29 us (2%)
    pallas_call x1, Pallas kernels, per_device(): pl.pallas_call(kernel, out_shape=out_shape, in_specs=[pl.BlockSpec(memory...  49.3 us
    pallas_call x1, Pallas kernels, per_device(): pl.pallas_call(pass_on, out_shape=out_shape, in_specs=[anywhere] * 4, out...  2.97 us

profile of v2, /device:TPU:1, one launch (start us, length us, event | category | flops | bytes accessed | tf_op | source)
XLA Modules:
  0.0 53.5 jit_solution(3107681957609677333)
XLA Ops:
  1.3 49.3 %grouped_attention_grads.1 = (bf16[128,768]{1,0:T(8,128)(2,1)}, bf16[128,768]{1,0:T(8,128)(2,1)}, bf16[128,768]{1,0:T(8,128)(2,1)}, f32[768,768]{1,0:T(8,128)}) custom-call(s32[1]{0:T(128)S(6)} %copy.10.kept_ref, bf16[128,768]{1,0:T(8,128)(2,1)} %bitcast.7, bf16[128,768]{1,0:T(8,128)(2,1)} %bitcast.8, bf16[128,768]{1,0:T(8,128)(2,1)} %bitcast.9, ...), custom_call_target="tpu_custom_call" | custom-call | tf_op jit(solution)/shard_map/grouped_attention_grads/pallas_call | solution.py:454
  50.6 3.0 %pass_on.1 = (bf16[128,768]{1,0:T(8,128)(2,1)}, bf16[128,768]{1,0:T(8,128)(2,1)}, bf16[128,768]{1,0:T(8,128)(2,1)}, f32[768,768]{1,0:T(8,128)}) custom-call(bf16[128,768]{1,0:T(8,128)(2,1)} %get-tuple-element.12.refs_0_, bf16[128,768]{1,0:T(8,128)(2,1)} %get-tuple-element.13.refs_1_, bf16[128,768]{1,0:T(8,128)(2,1)} %get-tuple-element.14.refs_2_, ...), custom_call_target="tpu_custom_call" | custom-call | tf_op jit(solution)/shard_map/pass_on/pallas_call | solution.py:497

commit v3 on v2

--- a/solution.py
+++ b/solution.py
@@ -42,8 +42,9 @@
 
 
 def kernel(
-    kept_ref, q_ref, k_ref, v_ref, g_ref, w_ref,
+    kept_ref, q_in, k_in, v_in, g_in, w_in,
     dq_ref, dk_ref, dv_ref, dw_ref,
+    q_ref, k_ref, v_ref, w_ref, load_sem,
     a_send, a_recv, a_back, a_ret, g_all, probs_ref, low_ref,
     b_send, b_recv, kv_all, dkv_send, dkv_recv, b_back, b_ret,
     pa_own, pa_send, pa_recv, pb_own, pb_send, pb_recv, za, tb, g1, g2, g3,
@@ -107,18 +108,18 @@
         for rm in range(2):
             greet(xm_peer(rx, rm))
 
+    loads = [
+        pltpu.make_async_copy(src, dst, load_sem.at[n])
+        for n, (src, dst) in enumerate(
+            ((k_in, k_ref), (q_in, q_ref), (v_in, v_ref), (g_in, g_all.at[pos]), (w_in, w_ref))
+        )
+    ]
+    for copy in loads:
+        copy.start()
     kept = kept_ref[0]
     far = pl.ds(HALF, HALF)
-    col_ok = jnp.where(seq * ROWS + iota((1, ROWS), 1) < kept, 1.0, 0.0)
-    grad = g_ref[...]
-    d_attn = (dot(w_ref[...], grad, NT) * col_ok).astype(BF16)
-    near = (turn(q_ref[:, :HALF]), turn(k_ref[:, :HALF]), turn(v_ref[:, :HALF]), d_attn[:HALF])
-    for d in range(4):
-        for t in range(4):
-            a_send[d, 96 * t : 96 * t + 96, :] = near[t][96 * d : 96 * d + 96]
-    a_recv[pos] = a_send[pos]
-    g_all[pos] = grad
-
+    for copy in loads[:4]:
+        copy.wait()
     r64 = iota((64, ROWS), 0)
     pick = one_hot(iota((64, ROWS), 1) == 16 * (r64 & 7) + (r64 >> 3))
     l_in = iota((64, HALF), 1) - HD * (iota((64, HALF), 0) >> 3)
@@ -129,17 +130,17 @@
     fold0 = one_hot(lane == feat)
     fold1 = one_hot(lane == feat + HD)
 
-    def dilated(block, dims=NN):
-        rows = dot(pick, block, dims)
+    def dilated(block):
+        rows = dot(pick, block)
         return jnp.where(own_lanes, rows, 0.0).astype(BF16)
 
     def tops(block):
         return block.reshape(8, 8, block.shape[-1])
 
-    far_ko = dot(dilated(k_ref[:, far]), fold0) + dot(dilated(d_attn[HALF:], NT), fold1)
+    far_k = dot(dilated(k_ref[:, far]), fold0)
     far_qv = dot(dilated(q_ref[:, far]), fold0) + dot(dilated(v_ref[:, far]), fold1)
-    far_g = dot(pick, grad)
-    b_send[:, :, :ROWS] = jnp.concatenate([tops(far_ko), tops(far_qv)], axis=1).astype(BF16)
+    far_g = dot(pick, g_all[pos])
+    b_send[:, :, :ROWS] = jnp.concatenate([tops(far_k), tops(far_qv)], axis=1).astype(BF16)
     b_send[:, :, ROWS:] = jnp.concatenate(
         [tops(far_g[:, :HALF]), tops(far_g[:, HALF:])], axis=1
     ).astype(BF16)
@@ -151,6 +152,15 @@
         send(b_send.at[(z + r) % 8], b_recv.at[z], b_ss.at[r - 1], b_rs.at[r - 1], z_peer(r))
         for r in (4, 3, 5, 2, 6, 1, 7)
     ]
+    g_across = send(g_all.at[pos], g_all.at[pos], gr_ss.at[0], gr_rs.at[0], across)
+    g_near = send(g_all.at[pos], g_all.at[pos], gr_ss.at[1], gr_rs.at[1], partner)
+
+    near = (turn(q_ref[:, :HALF]), turn(k_ref[:, :HALF]), turn(v_ref[:, :HALF]))
+    for d in range(4):
+        for t in range(3):
+            a_send[d, 96 * t : 96 * t + 96, :] = near[t][96 * d : 96 * d + 96]
+    a_recv[pos] = a_send[pos]
+
     a_in = [
         send(
             a_send.at[(pos + r) % 4], a_recv.at[pos],
@@ -158,25 +168,22 @@
         )
         for r in range(1, 4)
     ]
-    g_across = send(g_ref, g_all.at[pos], gr_ss.at[0], gr_rs.at[0], across)
-    g_near = send(g_ref, g_all.at[pos], gr_ss.at[1], gr_rs.at[1], partner)
-
     arrived(b_in)
     rows = b_recv[:, :, :ROWS].astype(F32)
-    ko = rows[:, :8, :].reshape(64, ROWS)
+    k_rows = rows[:, :8, :].reshape(64, ROWS)
     qv = rows[:, 8:, :].reshape(64, ROWS)
     lane64 = iota((64, ROWS), 1)
     left = lane64 < HD
     right = (lane64 >= HD) & (lane64 < 2 * HD)
-    kv_all[tee] = jnp.where(left, ko, jnp.where(right, qv, 0.0)).astype(BF16)
+    kv_all[tee] = jnp.where(left, k_rows, jnp.where(right, qv, 0.0)).astype(BF16)
     kv_in = [
         send(kv_all.at[tee], kv_all.at[tee], kv_ss.at[r - 1], kv_rs.at[r - 1], plane_peer(r))
         for r in range(1, 8)
     ]
     q_rows = jnp.where(left, qv, 0.0).astype(BF16)
-    o_rows = jnp.where(right, ko, 0.0).astype(BF16)
     q_cols = turn(q_rows)
-    o_cols = turn(o_rows)
+
+    loads[4].wait()
 
     arrived(a_in)
     at = first * ROWS
@@ -212,11 +219,10 @@
     far_probs = softmax(dot(kv, q_cols), far_key_ok)
     far_low = far_probs.astype(BF16)
     attn_far = (dot(kv_cols, far_low) * far_row_ok).astype(BF16)
-    g_rows = b_recv[:, :, ROWS:].astype(F32)
+    rows = b_recv[:, :, ROWS:].astype(F32)
+    far_g = [rows[:, 8 * i : 8 * i + 8, :].reshape(64, HALF).astype(BF16) for i in range(2)]
     for i in range(2):
-        block = dot(
-            attn_far[HD : 2 * HD], g_rows[:, 8 * i : 8 * i + 8, :].reshape(64, HALF).astype(BF16)
-        )
+        block = dot(attn_far[HD : 2 * HD], far_g[i])
         for half in range(2):
             piece = block[24 * half : 24 * half + 24]
             pb_own[2 * half + i] = piece
@@ -242,6 +248,13 @@
         for rx, rm in ((2, 1), (1, 1), (3, 1), (2, 0), (1, 0), (3, 0), (0, 1))
     ]
 
+    w_at = pl.multiple_of(HALF + HD * z, 16)
+    d_attn = sum(
+        dot(w_ref[pl.ds(w_at, HD), HALF * i : HALF * i + HALF], far_g[i], NT) for i in range(2)
+    )
+    pad = jnp.zeros((HD, 64), F32)
+    o_cols = jnp.concatenate([pad, d_attn * far_row_ok, pad[: ROWS - 2 * HD]], axis=0).astype(BF16)
+    o_rows = turn(o_cols)
     row_dot = jnp.sum(o_cols.astype(F32) * attn_far.astype(F32), axis=0, keepdims=True)
     far_ds = (far_probs * (dot(kv, o_cols) - row_dot)).astype(BF16)
     far_dq = jnp.transpose(dot(kv_cols, far_ds) * SCALING)
@@ -267,8 +280,12 @@
         for r in range(1, 8)
     ]
 
+    w_at = pl.multiple_of(96 * pos, 96)
+    d_attn = (dot(w_ref[pl.ds(w_at, 96), :], g_all[...].reshape(SEG, WIDTH), NT) * row_ok).astype(BF16)
+
     def near_back(h):
-        q_t, k_t, v_t, o_t = (head_rows(t, h) for t in range(4))
+        q_t, k_t, v_t = (head_rows(t, h) for t in range(3))
+        o_t = d_attn[HD * h : HD * h + HD]
         row_dot = jnp.sum(o_t.astype(F32) * attn_near[h].astype(F32), axis=0, keepdims=True)
         d_scores = (probs_ref[h] * (dot(turn(v_t), o_t) - row_dot)).astype(BF16)
         outs = (
@@ -425,23 +442,16 @@
 
 
 def pass_on(*refs):
-    ins, outs, held, in_sem, out_sem = refs[:4], refs[4:8], refs[8:12], refs[12], refs[13]
-    chunks = [(i, slice(None)) for i in range(3)]
-    chunks += [(3, pl.ds(192 * j, 192)) for j in range(4)]
-    arriving = []
-    for n, (i, at) in enumerate(chunks):
-        arriving.append(
-            pltpu.make_async_copy(ins[i].at[at], held[i].at[at], in_sem.at[n])
-        )
-        arriving[-1].start()
-    leaving = []
-    for n, (i, at) in enumerate(chunks):
-        arriving[n].wait()
-        leaving.append(
-            pltpu.make_async_copy(held[i].at[at], outs[i].at[at], out_sem.at[n])
-        )
-        leaving[-1].start()
-    for copy in leaving:
+    ins, outs, sem = refs[:4], refs[4:8], refs[8]
+    copies = [
+        pltpu.make_async_copy(ins[i].at[at], outs[i].at[at], sem.at[n])
+        for n, (i, at) in enumerate(
+            [(3, pl.ds(192 * j, 192)) for j in range(4)] + [(i, slice(None)) for i in range(3)]
+        )
+    ]
+    for copy in copies:
+        copy.start()
+    for copy in copies:
         copy.wait()
 
 
@@ -453,12 +463,17 @@
     out_shape = (block, block, block, jax.ShapeDtypeStruct((WIDTH, WIDTH), F32))
     outs = pl.pallas_call(
         kernel,
-        out_shape=out_shape,
-        in_specs=[pl.BlockSpec(memory_space=pltpu.SMEM)] + [vmem] * 5,
+        out_shape=tuple(pltpu.VMEM(s.shape, s.dtype) for s in out_shape),
+        in_specs=[pl.BlockSpec(memory_space=pltpu.SMEM)] + [anywhere] * 5,
         out_specs=(vmem,) * 4,
         scratch_shapes=[
-            pltpu.VMEM((4, HALF, ROWS), BF16),
-            pltpu.VMEM((4, HALF, ROWS), BF16),
+            pltpu.VMEM((ROWS, WIDTH), BF16),
+            pltpu.VMEM((ROWS, WIDTH), BF16),
+            pltpu.VMEM((ROWS, WIDTH), BF16),
+            pltpu.VMEM((WIDTH, WIDTH), BF16),
+            dma((5,)),
+            pltpu.VMEM((4, 288, ROWS), BF16),
+            pltpu.VMEM((4, 288, ROWS), BF16),
             pltpu.VMEM((4, 288, ROWS), BF16),
             pltpu.VMEM((4, 288, ROWS), BF16),
             pltpu.VMEM((4, ROWS, WIDTH), BF16),
@@ -497,12 +512,11 @@
     outs = pl.pallas_call(
         pass_on,
         out_shape=out_shape,
-        in_specs=[anywhere] * 4,
+        in_specs=[vmem] * 4,
         out_specs=(anywhere,) * 4,
-        scratch_shapes=[pltpu.VMEM(s.shape, s.dtype) for s in out_shape]
-        + [dma((7,)), dma((7,))],
+        scratch_shapes=[dma((7,))],
         name="pass_on",
-    )(*outs)
+    )(*[pltpu.with_memory_space_constraint(out, pltpu.VMEM) for out in outs])
     return (outs[0][None], outs[1][None], outs[2][None], outs[3])
 
 

time: 53.7 us -> 48.2 us (0.90)
  Pallas kernels: 52.2 us -> 46.8 us
    pallas_call x2, Pallas kernels: 52.2 us -> 46.8 us  [the longest x1 45.2 us: per_device(): pl.pallas_call(kernel, out_shape=tuple((pltpu.VMEM(s.shape, s.dtype) for...]
where the time goes in v3:
time: 48.2 us; the launch traced here: 48.1 us
  Pallas kernels  46.8 us (97%)
  between operations  1.29 us (3%)
    pallas_call x1, Pallas kernels, per_device(): pl.pallas_call(kernel, out_shape=tuple((pltpu.VMEM(s.shape, s.dtype) for...  45.2 us
    pallas_call x1, Pallas kernels, per_device(): pl.pallas_call(pass_on, out_shape=out_shape, in_specs=[vmem] * 4, out_spe...  1.65 us

profile of v3, /device:TPU:1, one launch (start us, length us, event | category | flops | bytes accessed | tf_op | source)
XLA Modules:
  0.0 48.1 jit_solution(3852626336672801263)
XLA Ops:
  1.3 45.2 %grouped_attention_grads.1 = (bf16[128,768]{1,0:T(8,128)(2,1)S(1)}, bf16[128,768]{1,0:T(8,128)(2,1)S(1)}, bf16[128,768]{1,0:T(8,128)(2,1)S(1)}, f32[768,768]{1,0:T(8,128)S(1)}) custom-call(s32[1]{0:T(128)S(6)} %copy.10.kept_ref, bf16[128,768]{1,0:T(8,128)(2,1)} %bitcast.7, bf16[128,768]{1,0:T(8,128)(2,1)} %bitcast.8, bf16[128,768]{1,0:T(8,128)(2,1)} %bitcast.9, ...), custom_call_target="tpu_custom_call" | custom-call | tf_op jit(solution)/shard_map/grouped_attention_grads/pallas_call | solution.py:464
  46.5 1.6 %pass_on.1 = (bf16[128,768]{1,0:T(8,128)(2,1)}, bf16[128,768]{1,0:T(8,128)(2,1)}, bf16[128,768]{1,0:T(8,128)(2,1)}, f32[768,768]{1,0:T(8,128)}) custom-call(bf16[128,768]{1,0:T(8,128)(2,1)S(1)} %get-tuple-element.12.refs_0_, bf16[128,768]{1,0:T(8,128)(2,1)S(1)} %get-tuple-element.13.refs_1_, bf16[128,768]{1,0:T(8,128)(2,1)S(1)} %get-tuple-element.14.refs_2_, ...), custom_call_target="tpu_custom_call" | custom-call | tf_op jit(solution)/shard_map/pass_on/pallas_call | solution.py:512
